TPU v7x, 128 devices: a whole 4x4x4 slice. The times are simulated.
128 devices in a mesh: req: 16 (over y, x), exp: 8 (over z, core).
Axes of the slice: x: 4, y: 4, z: 4, core: 2. Of those that a mesh axis runs over, the one named last changes fastest.
Arguments:
- attention_out: bfloat16 [2048, 4096], P('req'), may hold values from -6 to 6
- residual: bfloat16 [2048, 4096], P('req', 'exp'), may hold values from -6 to 6
- w_out: bfloat16 [4096, 4096], P('req', 'exp'), may hold values from -0.09375 to 0.09375
- router_w: float32 [4096, 8], P('exp'), may hold values from -0.09375 to 0.09375
- norm_gain: float32 [4096], P('exp'), may hold values from 0.5 to 1.5
- page_pool: bfloat16 [4096, 8, 2048], P('req', None, 'exp'), may hold values from -6 to 6
- page_table: int32 [2048, 2], P('req'), may hold values from 0 to 255, as said below
- cache_len: int32 [2048], P('req'), may hold values from 1 to 16
- came_from: int32 [2048], replicated, may hold values from 0 to 2047, as said below
- routes: int32 [2048, 2], P('req'), may hold values from 0 to 7, all different within a row; in each aligned block of 128 rows (0 to 127, 128 to 255, ...) at most 64 rows name the same one
- w_gate: bfloat16 [16, 4096, 7168], P('req', None, 'exp'), as said below
- w_up: bfloat16 [16, 4096, 7168], P('req', None, 'exp'), as said below
- w_down: bfloat16 [16, 7168, 4096], P('req', 'exp'), as said below
Outputs:
- mixed: float32 [2048, 4096], P('req', 'exp')
- new_pages: bfloat16 [2048, 2, 8, 2048], P('req', None, None, 'exp')
Inputs may be any that keep to these rules, and one draw needn't show every extreme that they name: page_table's entries for the requests of one req group are distinct. came_from is a permutation; from each req group 4 rows go to each of the other 15 groups, each group receives 4 rows from each of them, and all other rows keep their place. `routes`: within the rows of one req group every expert is named by at most 64 rows, and some expert by exactly 64 rows in some group. `w_gate`: slices e and e + 8 along the first dimension are equal. `w_up`: slices e and e + 8 along the first dimension are equal. `w_down`: slices e and e + 8 along the first dimension are equal.
All inputs are finite; a program needn't handle non-finite values.
Results may differ from a plain program's by a relative error of at most 0.0055.
Values may be sent and summed in bfloat16 or wider, within the bound.
A program may use at most 128 MiB of HBM per device.

v0:
```python
import jax
import jax.numpy as jnp
from jax import lax
from jax.sharding import PartitionSpec as P

D = 4096
CAP = 32
MIG_PAIR = 4
EPSILON = 1e-05


def pick_rows(source, row_index, live_slot):
    taken_rows = jnp.take(source, row_index, axis=0)
    return jnp.where(live_slot[:, None], taken_rows, jnp.zeros((), source.dtype))


def body(
    attention_out,
    residual,
    w_out,
    router_w,
    norm_gain,
    page_pool,
    page_table,
    cache_len,
    came_from,
    routes,
    w_gate,
    w_up,
    w_down,
):
    groups = lax.axis_size("req")
    own_group = lax.axis_index("req")
    row_req = attention_out.shape[0]
    rows_all = came_from.shape[0]
    pages_req = page_table.shape[1]
    page_len = page_pool.shape[1]
    kv_slice = page_pool.shape[2]
    experts = groups // 2
    targets = jnp.arange(groups, dtype=jnp.int32)
    local_ids = jnp.arange(row_req, dtype=jnp.int32)
    dest_of = (
        jnp.zeros((rows_all,), jnp.int32).at[came_from].set(jnp.arange(rows_all, dtype=jnp.int32))
    )
    dest_group = dest_of // row_req
    dest_hot = (
        (dest_group[:, None] == targets[None, :]).astype(jnp.int32).reshape(groups, row_req, groups)
    )
    pair_rank = jnp.sum((jnp.cumsum(dest_hot, axis=1) - dest_hot) * dest_hot, axis=2).reshape(
        rows_all
    )
    own_dest = lax.dynamic_slice_in_dim(dest_group, own_group * row_req, row_req)
    own_rank = lax.dynamic_slice_in_dim(pair_rank, own_group * row_req, row_req)
    chosen_send = (
        (own_dest[None, None, :] == targets[:, None, None])
        & (own_rank[None, None, :] == jnp.arange(MIG_PAIR, dtype=jnp.int32)[None, :, None])
        & (targets[:, None, None] != own_group)
    )
    send_index = jnp.sum(jnp.where(chosen_send, local_ids[None, None, :], 0), axis=2).reshape(-1)
    send_live = jnp.any(chosen_send, axis=2).reshape(-1)
    page_rows = jnp.take(page_pool, page_table.reshape(-1), axis=0).reshape(
        row_req, pages_req, page_len, kv_slice
    )
    position = (
        jnp.arange(pages_req, dtype=jnp.int32)[:, None] * page_len
        + jnp.arange(page_len, dtype=jnp.int32)[None, :]
    )
    kept_mask = position[None, :, :] < cache_len[:, None, None]
    page_rows = jnp.where(kept_mask[..., None], page_rows, jnp.zeros((), page_rows.dtype)).reshape(
        row_req, -1
    )
    moved_attn, moved_resid, moved_pages = (
        lax.all_to_all(
            pick_rows(attention_out, send_index, send_live),
            "req",
            split_axis=0,
            concat_axis=0,
            tiled=True,
        ),
        lax.all_to_all(
            pick_rows(residual, send_index, send_live),
            "req",
            split_axis=0,
            concat_axis=0,
            tiled=True,
        ),
        lax.all_to_all(
            pick_rows(page_rows, send_index, send_live),
            "req",
            split_axis=0,
            concat_axis=0,
            tiled=True,
        ),
    )
    new_source = lax.dynamic_slice_in_dim(came_from, own_group * row_req, row_req)
    source_group = new_source // row_req
    stays_home = source_group == own_group
    arrival = jnp.where(
        stays_home,
        new_source - own_group * row_req,
        row_req + source_group * MIG_PAIR + jnp.take(pair_rank, new_source),
    )
    attn_new = jnp.take(jnp.concatenate([attention_out, moved_attn], axis=0), arrival, axis=0)
    resid_new = jnp.take(jnp.concatenate([residual, moved_resid], axis=0), arrival, axis=0)
    new_pages = jnp.take(
        jnp.concatenate([page_rows, moved_pages], axis=0), arrival, axis=0
    ).reshape(row_req, pages_req, page_len, kv_slice)
    projected = jnp.dot(
        attn_new,
        lax.all_gather(w_out, "req", axis=0, tiled=True),
        preferred_element_type=jnp.float32,
    )
    hidden = resid_new.astype(jnp.float32) + projected
    squares = jnp.sum(hidden * hidden, axis=1)
    scaled = hidden * norm_gain[None, :]
    total_sq = lax.psum(squares, "exp")
    inverse = lax.rsqrt(total_sq / D + EPSILON)
    normed = scaled * inverse[:, None]
    logits = lax.psum(jnp.dot(normed, router_w, precision=lax.Precision.HIGHEST), "exp")
    normed_rows = normed.astype(jnp.bfloat16)
    expert_ids = jnp.arange(experts, dtype=jnp.int32)
    chosen = jnp.sum(
        jnp.where(routes[:, :, None] == expert_ids[None, None, :], logits[:, None, :], 0.0), axis=2
    )
    gate_first = jax.nn.sigmoid(chosen[:, 0] - chosen[:, 1])
    gate_second = jax.nn.sigmoid(chosen[:, 1] - chosen[:, 0])
    flat_routes = routes.reshape(-1)
    expert_hot = (flat_routes[:, None] == expert_ids[None, :]).astype(jnp.int32)
    expert_rank = jnp.sum((jnp.cumsum(expert_hot, axis=0) - expert_hot) * expert_hot, axis=1)
    target_dev = flat_routes + experts * (expert_rank % 2)
    slot_index = expert_rank // 2
    assign_ids = jnp.arange(flat_routes.shape[0], dtype=jnp.int32)
    chosen_slot = (target_dev[None, None, :] == targets[:, None, None]) & (
        slot_index[None, None, :] == jnp.arange(CAP, dtype=jnp.int32)[None, :, None]
    )
    slot_source = jnp.sum(
        jnp.where(chosen_slot, assign_ids[None, None, :] // 2, 0), axis=2
    ).reshape(-1)
    slot_live = jnp.any(chosen_slot, axis=2).reshape(-1)
    outgoing = pick_rows(normed_rows, slot_source, slot_live)
    arrived = lax.all_to_all(outgoing, "req", split_axis=0, concat_axis=0, tiled=True)
    rows_full = lax.all_gather(arrived, "exp", axis=1, tiled=True)
    gate_h = jnp.dot(rows_full, w_gate[0], preferred_element_type=jnp.float32)
    up_h = jnp.dot(rows_full, w_up[0], preferred_element_type=jnp.float32)
    active = (jax.nn.silu(gate_h) * up_h).astype(jnp.bfloat16)
    partial_value = lax.optimization_barrier(
        jnp.dot(active, w_down[0], preferred_element_type=jnp.float32).astype(jnp.bfloat16)
    )
    lookup = target_dev * CAP + slot_index
    returned = lax.all_to_all(partial_value, "req", split_axis=0, concat_axis=0, tiled=True)
    taken_rows = jnp.take(returned, lookup, axis=0).reshape(row_req, 2, -1)
    weighted = gate_first[:, None] * taken_rows[:, 0].astype(jnp.float32) + gate_second[
        :, None
    ] * taken_rows[:, 1].astype(jnp.float32)
    expert_part = lax.psum_scatter(
        weighted.astype(jnp.bfloat16), "exp", scatter_dimension=1, tiled=True
    ).astype(jnp.float32)
    mixed = hidden + expert_part
    return (mixed, new_pages)


def solution(mesh):
    in_specs = (
        P("req", None),
        P("req", "exp"),
        P("req", "exp"),
        P("exp", None),
        P("exp"),
        P("req", None, "exp"),
        P("req", None),
        P("req"),
        P(),
        P("req", None),
        P("req", None, "exp"),
        P("req", None, "exp"),
        P("req", "exp", None),
    )
    out_specs = (P("req", "exp"), P("req", None, None, "exp"))
    return jax.shard_map(body, mesh=mesh, in_specs=in_specs, out_specs=out_specs, check_vma=False)
```

profile of v0, /device:TPU:0, one launch (start us, length us, event | category | flops | bytes accessed | tf_op | source)
XLA Modules:
  0.0 285.6 jit_solution(12334850241228818001)
XLA Ops:
  7.2 0.7 all-gather.3.cloned.1.call-update
  7.9 0.7 compare_select_fusion.1
  8.6 8.0 %scatter_custom_fusion = s32[2048]{0:T(1024)S(1)} fusion(s32[2048]{0:T(1024)S(1)} %compare_select_fusion.1, s32[2048]{0:T(1024)S(1)} %iota.72, s32[]{:T(128)} %constant.182.clone.1), kind=kCustom, calls=%fused_computation.92 | custom fusion | bytes 8196 | tf_op jit(solution)/shard_map/scatter | solution.py:43
  16.9 2.8 select_reduce_fusion
  20.7 1.6 gather_fusion.1
  22.4 0.7 select_select_fusion.4
  23.1 7.1 %all-to-all-start = ((bf16[16,4,512]{2,1,0:T(4,128)(2,1)}), bf16[16,4,512]{2,1,0:T(4,128)(2,1)S(1)}, u32[]{:S(2)}, u32[]{:S(2)}) async-start(bf16[16,4,512]{2,1,0:T(4,128)(2,1)} %select_select_fusion.4), calls=%async_computation | async-start | bytes 131072 | tf_op jit(solution)/shard_map/all_to_all | solution.py:80
  30.3 0.8 copy.122
  31.5 0.8 copy.131
  32.3 0.7 compare_and_fusion.2
  33.1 0.6 reduce-window.6
  34.6 0.8 compare_select_fusion.15
  35.3 1.1 gather_fusion
  36.9 0.4 broadcast_in_dim.226
  37.7 0.4 broadcast_in_dim.228
  38.1 1.1 copy.133
  39.2 1.7 gather_fusion.5
  41.0 2.4 gather.47
  43.4 0.9 gather_fusion.6
  44.2 1.6 select_select_fusion
  45.8 0.9 gather_fusion.8
  46.8 1.0 select_select_fusion.1
  47.8 1.0 all_to_all.38
  48.8 0.8 compare_and_fusion.5
  49.6 7.2 %all-to-all-start.1 = ((bf16[16,4,4096]{2,1,0:T(4,128)(2,1)}), bf16[16,4,4096]{2,1,0:T(4,128)(2,1)S(1)}, u32[]{:S(2)}, u32[]{:S(2)}) async-start(bf16[16,4,4096]{2,1,0:T(4,128)(2,1)} %all_to_all.38), calls=%async_computation.1 | async-start | bytes 1048576 | tf_op jit(solution)/shard_map/all_to_all | solution.py:73
  57.4 0.8 gather_fusion.2
  58.2 13.6 %all-to-all-done.1 = bf16[16,4,4096]{2,1,0:T(4,128)(2,1)S(1)} async-done(((bf16[16,4,4096]{2,1,0:T(4,128)(2,1)}), bf16[16,4,4096]{2,1,0:T(4,128)(2,1)S(1)}, u32[]{:S(2)}, u32[]{:S(2)}) %all-to-all-start.1) | async-done | bytes 524320 | tf_op jit(solution)/shard_map/all_to_all | solution.py:73
  72.2 1.2 gather_fusion.7
  73.4 3.0 %multiply_reduce_fusion = (f32[128]{0:T(128)S(1)}, f32[128,512]{1,0:T(8,128)S(1)}) fusion(bf16[4096,512]{1,0:T(8,128)(2,1)} %all-gather.3.cloned.1.call-done, bf16[128,4096]{1,0:T(8,128)(2,1)S(1)} %gather_fusion.7, pred[128]{0:T(512)(128)(4,1)S(1)} %get-tuple-element.4, bf16[128,512]{1,0:T(8,128)(2,1)S(1)} %gather_fusion.2), kind=kOutput, calls=%fused_computation.47 | convolution fusion | flops 537722752 | bytes 5636736 | tf_op jit(solution)/shard_map/dot_general | solution.py:108
  76.4 14.3 %psum.14 = f32[128]{0:T(128)S(1)} all-reduce(f32[128]{0:T(128)S(1)} %get-tuple-element.14), channel_id=1, replica_groups=mesh['req'=16,'exp'=8] {'exp'}, use_global_device_ids=true, to_apply=%region_6.9 | all-reduce | flops 128 | bytes 1024 | tf_op jit(solution)/shard_map/psum | solution.py:116
  90.8 2.0 gather_fusion.3
  93.0 13.6 %all_to_all.54 = bf16[16,32,512]{2,1,0:T(8,128)(2,1)} all-to-all(bf16[16,32,512]{2,1,0:T(8,128)(2,1)S(1)} %select_select_fusion.3), channel_id=1, replica_groups=mesh['req'=16,'exp'=8] {'req'}, dimensions={0} | all-to-all | bytes 1048576 | tf_op jit(solution)/shard_map/all_to_all | solution.py:141
  106.6 28.7 %all-gather.5.cloned.1.call-done = bf16[512,4096]{1,0:T(8,128)(2,1)} async-done(((bf16[512,512]{1,0:T(8,128)(2,1)}), bf16[512,4096]{1,0:T(8,128)(2,1)}) %all-gather.5.cloned.1.call-update) | async-done | bytes 4194320 | tf_op jit(solution)/shard_map/all_gather | solution.py:142
  135.3 9.8 %fusion.4 = f32[512,896]{1,0:T(8,128)S(1)} fusion(bf16[512,4096]{1,0:T(8,128)(2,1)} %all-gather.5.cloned.1.call-done, bf16[1,4096,896]{2,1,0:T(8,128)(2,1)} %param.27), kind=kOutput, calls=%fused_computation.15 | convolution fusion | flops 3758096384 | bytes 13369344 | tf_op jit(solution)/shard_map/dot_general | solution.py:143
  145.1 16.3 %fusion.6 = bf16[512,4096]{1,0:T(8,128)(2,1)} fusion(bf16[1,896,4096]{2,1,0:T(8,128)(2,1)} %param.29, f32[512,896]{1,0:T(8,128)S(1)} %fusion.4, bf16[512,4096]{1,0:T(8,128)(2,1)} %all-gather.5.cloned.1.call-done, bf16[1,4096,896]{2,1,0:T(8,128)(2,1)} %param.28), kind=kOutput, calls=%fused_computation.17 | convolution fusion | flops 7521042432 | bytes 24903680 | tf_op jit(solution)/shard_map/dot_general | solution.py:147
  161.4 7.0 %all-to-all-start.3 = ((bf16[16,32,4096]{2,1,0:T(8,128)(2,1)}), bf16[16,32,4096]{2,1,0:T(8,128)(2,1)}, u32[]{:S(2)}, u32[]{:S(2)}) async-start(bf16[16,32,4096]{2,1,0:T(8,128)(2,1)} %bitcast.67), calls=%async_computation.3 | async-start | bytes 8388608 | tf_op jit(solution)/shard_map/all_to_all | solution.py:150
  169.3 13.8 %psum.15 = f32[128,8]{0,1:T(8,128)S(1)} all-reduce(f32[128,8]{0,1:T(8,128)S(1)} %fusion.25), channel_id=1, replica_groups=mesh['req'=16,'exp'=8] {'exp'}, use_global_device_ids=true, to_apply=%region_7.10 | all-reduce | flops 1024 | bytes 8192 | tf_op jit(solution)/shard_map/psum | solution.py:119
  183.1 49.0 %all-to-all-done.3 = bf16[16,32,4096]{2,1,0:T(8,128)(2,1)} async-done(((bf16[16,32,4096]{2,1,0:T(8,128)(2,1)}), bf16[16,32,4096]{2,1,0:T(8,128)(2,1)}, u32[]{:S(2)}, u32[]{:S(2)}) %all-to-all-start.3) | async-done | bytes 4194336 | tf_op jit(solution)/shard_map/all_to_all | solution.py:150
  232.1 6.6 %gather_fusion.4 = bf16[256,4096]{1,0:T(8,128)(2,1)S(1)} fusion(bf16[512,4096]{1,0:T(8,128)(2,1)} %bitcast.13, s32[1024]{0:T(1024)S(1)} %pad_clamp_fusion.1), kind=kCustom, calls=%fused_computation.8 | custom fusion | bytes 4195328 | tf_op jit(solution)/shard_map/jit(_take)/gather | solution.py:151
  238.8 2.7 gather.45
  241.4 4.0 %copy_select_fusion = bf16[128,2,4096]{2,0,1:T(8,128)(2,1)S(1)} fusion(bf16[128,2,4096]{2,1,0:T(2,128)(2,1)} %gather.45, pred[128,2]{0,1:T(4,128)(4,1)S(1)} %compare_and_fusion.3), kind=kLoop, calls=%fused_computation.22 | loop fusion | flops 1048576 | bytes 4194560 | tf_op jit(solution)/shard_map/jit(_take)/select_n | solution.py:151
  245.5 1.5 fusion.10
  247.2 15.8 %all_to_all.55 = bf16[16,4,4096]{2,1,0:T(4,128)(2,1)S(1)} all-to-all(bf16[16,4,4096]{2,1,0:T(4,128)(2,1)S(1)} %all_to_all.46), channel_id=1, replica_groups=mesh['req'=16,'exp'=8] {'req'}, dimensions={0} | all-to-all | bytes 1048576 | tf_op jit(solution)/shard_map/all_to_all | solution.py:87
  263.3 2.2 gather_fusion.9
  265.5 1.4 broadcast_select_fusion
  266.9 1.2 copy.134
  268.1 9.3 %reduce-scatter.2.cloned.1.call-done = bf16[128,512]{1,0:T(8,128)(2,1)} async-done(((bf16[128,4096]{1,0:T(8,128)(2,1)}), bf16[128,512]{1,0:T(8,128)(2,1)}) %reduce-scatter.2.cloned.1.call-update) | async-done | bytes 131088 | tf_op jit(solution)/shard_map/reduce_scatter | solution.py:155
  277.4 1.6 convert_add_fusion
  (99 shorter events, 5.9 us)
Async XLA Ops:
  7.2 32.1 %copy-start = (bf16[256,8,256]{2,1,0:T(8,128)(2,1)S(1)}, bf16[256,8,256]{2,1,0:T(8,128)(2,1)}, u32[]{:S(2)}) copy-start(bf16[256,8,256]{2,1,0:T(8,128)(2,1)} %param.22) | copy-start | bytes 3145732
  7.2 29.5 %copy-start.10 = (s32[128]{0:T(128)S(1)}, s32[128]{0:T(128)}, u32[]{:S(2)}) copy-start(s32[128]{0:T(128)} %param.24) | copy-start | bytes 1540
  7.2 66.2 %all-gather.3.cloned.1.call-start = ((), (), s32[]{:S(2)}) async-start(), calls=%async_computation.6 | async-start | bytes 4456448 | tf_op jit(solution)/shard_map/all_gather | solution.py:110
  23.1 26.5 %all-to-all-start = ((bf16[16,4,512]{2,1,0:T(4,128)(2,1)}), bf16[16,4,512]{2,1,0:T(4,128)(2,1)S(1)}, u32[]{:S(2)}, u32[]{:S(2)}) async-start(bf16[16,4,512]{2,1,0:T(4,128)(2,1)} %select_select_fusion.4), calls=%async_computation | async-start | bytes 131072 | tf_op jit(solution)/shard_map/all_to_all | solution.py:80
  39.2 4.1 %copy-start.4 = (bf16[128,4096]{1,0:T(8,128)(2,1)S(1)}, bf16[128,4096]{1,0:T(8,128)(2,1)}, u32[]{:S(2)}) copy-start(bf16[128,4096]{1,0:T(8,128)(2,1)} %param.17) | copy-start | bytes 3145732
  45.8 1.0 copy-start.2
  46.8 10.5 %copy-start.5 = (bf16[128,512]{1,0:T(8,128)(2,1)S(1)}, bf16[128,512]{1,0:T(8,128)(2,1)}, u32[]{:S(2)}) copy-start(bf16[128,512]{1,0:T(8,128)(2,1)} %param.18) | copy-start | bytes 393220
  49.6 22.2 %all-to-all-start.1 = ((bf16[16,4,4096]{2,1,0:T(4,128)(2,1)}), bf16[16,4,4096]{2,1,0:T(4,128)(2,1)S(1)}, u32[]{:S(2)}, u32[]{:S(2)}) async-start(bf16[16,4,4096]{2,1,0:T(4,128)(2,1)} %all_to_all.38), calls=%async_computation.1 | async-start | bytes 1048576 | tf_op jit(solution)/shard_map/all_to_all | solution.py:73
  56.9 78.5 %all-gather.5.cloned.1.call-start = ((), (), s32[]{:S(2)}) async-start(), calls=%async_computation.7 | async-start | bytes 4718592 | tf_op jit(solution)/shard_map/all_gather | solution.py:142
  73.4 17.4 %copy-start.9 = (f32[512]{0:T(512)S(1)}, f32[512]{0:T(512)}, u32[]{:S(2)}) copy-start(f32[512]{0:T(512)} %param.21) | copy-start | bytes 6148
  161.4 7.5 %copy-start.8 = (s32[128,2]{0,1:T(2,128)S(1)}, s32[128,2]{0,1:T(2,128)}, u32[]{:S(2)}) copy-start(s32[128,2]{0,1:T(2,128)} %param.26) | copy-start | bytes 3076
  161.4 7.5 %copy-start.7 = (f32[512,8]{0,1:T(8,128)S(1)}, f32[512,8]{0,1:T(8,128)}, u32[]{:S(2)}) copy-start(f32[512,8]{0,1:T(8,128)} %param.20) | copy-start | bytes 49156
  161.4 70.7 %all-to-all-start.3 = ((bf16[16,32,4096]{2,1,0:T(8,128)(2,1)}), bf16[16,32,4096]{2,1,0:T(8,128)(2,1)}, u32[]{:S(2)}, u32[]{:S(2)}) async-start(bf16[16,32,4096]{2,1,0:T(8,128)(2,1)} %bitcast.67), calls=%async_computation.3 | async-start | bytes 8388608 | tf_op jit(solution)/shard_map/all_to_all | solution.py:150
  168.4 109.0 %reduce-scatter.2.cloned.1.call-start = ((), (), s32[]{:S(2)}) async-start(), calls=%async_computation.8 | async-start | bytes 1179648 | tf_op jit(solution)/shard_map/reduce_scatter | solution.py:155
  245.4 1.5 copy-start.6
  246.9 16.2 %copy-start.3 = (bf16[128,4096]{1,0:T(8,128)(2,1)S(1)}, bf16[128,4096]{1,0:T(8,128)(2,1)}, u32[]{:S(2)}) copy-start(bf16[128,4096]{1,0:T(8,128)(2,1)} %copy-done.2) | copy-start | bytes 3145732
  263.3 15.8 %copy-start.1 = (bf16[256,8,256]{2,1,0:T(8,128)(2,1)S(1)}, bf16[256,8,256]{2,1,0:T(8,128)(2,1)}, u32[]{:S(2)}) copy-start(bf16[256,8,256]{2,1,0:T(8,128)(2,1)} %param.22) | copy-start | bytes 3145732
Sparse Core Ops, SparseCore 0:
  10.2 59.3 all-gather.2
  106.7 28.5 all-gather.4
  247.1 30.3 reduce-scatter.1
where the time goes:
time: 286 us
  waiting for transfers between devices  101 us (35%)
  blocking collectives  57.5 us (20%)
  local copies, waits for them, and re-layouts  40.8 us (14%)
  matrix products  29.5 us (10%)
  starting transfers between devices  21.5 us (8%)
  other arithmetic  20.6 us (7%)
  between operations  14.2 us (5%)
    all_to_all x1, waiting for transfers between devices, body(): lax.all_to_all(partial_value, 'req', split_axis=0, concat_axis=0, tiled=T...  49 us
    all_gather x1, waiting for transfers between devices, body(): rows_full = lax.all_gather(arrived, 'exp', axis=1, tiled=True)  28.7 us
    dot_general x1, matrix products, body(): jnp.dot(active, w_down[0], preferred_element_type=jnp.float32)  16.3 us
    all_to_all x1, blocking collectives, body(): lax.all_to_all(pick_rows(page_rows, send_index, send_live), 'req', split_...  15.8 us
    psum x1, blocking collectives, body(): total_sq = lax.psum(squares, 'exp')  14.3 us
    psum x1, blocking collectives, body(): lax.psum(jnp.dot(normed, router_w, precision=lax.Precision.HIGHEST), 'exp')  13.8 us
    all_to_all x1, waiting for transfers between devices, body(): lax.all_to_all(pick_rows(attention_out, send_index, send_live), 'req', sp...  13.6 us
    all_to_all x1, blocking collectives, body(): lax.all_to_all(outgoing, 'req', split_axis=0, concat_axis=0, tiled=True)  13.6 us
  transfers between devices with their start and end apart: 6, of which 4 were waited for; matrix products, arithmetic and copies ran while one was open for 15% of the time, Pallas kernels for 0%

commit v1 on v0

--- a/solution.py
+++ b/solution.py
@@ -1,12 +1,30 @@
+import functools
 import jax
 import jax.numpy as jnp
 from jax import lax
 from jax.sharding import PartitionSpec as P
+from jax.lax import all_to_all, psum
 
 D = 4096
 CAP = 32
 MIG_PAIR = 4
 EPSILON = 1e-05
+
+
+def inputs_cut(here_x, out_dim):
+    y1 = jnp.concatenate(
+        all_to_all(
+            jnp.stack([here_x for _ in range(psum(1, "exp"))], axis=0),
+            "exp",
+            split_axis=0,
+            concat_axis=0,
+        ),
+        axis=out_dim,
+    )
+    return y1
+
+
+resolve_cubes = functools.partial(inputs_cut, out_dim=1)
 
 
 def pick_rows(source, row_index, live_slot):
@@ -139,7 +157,7 @@
     slot_live = jnp.any(chosen_slot, axis=2).reshape(-1)
     outgoing = pick_rows(normed_rows, slot_source, slot_live)
     arrived = lax.all_to_all(outgoing, "req", split_axis=0, concat_axis=0, tiled=True)
-    rows_full = lax.all_gather(arrived, "exp", axis=1, tiled=True)
+    rows_full = resolve_cubes(arrived)
     gate_h = jnp.dot(rows_full, w_gate[0], preferred_element_type=jnp.float32)
     up_h = jnp.dot(rows_full, w_up[0], preferred_element_type=jnp.float32)
     active = (jax.nn.silu(gate_h) * up_h).astype(jnp.bfloat16)

time: 286 us -> 307 us (1.073)
  blocking collectives: 57.5 us -> 109 us
  waiting for transfers between devices: 101 us -> 72.4 us
    all_to_all x0 -> x1, blocking collectives: none -> 53.2 us  [inputs_cut(): all_to_all(jnp.stack([here_x for _ in range(psum(1, 'exp'))], axis=0), 'e...]
    all_gather x1 -> x0, waiting for transfers between devices: 28.7 us -> none  [body(): rows_full = lax.all_gather(arrived, 'exp', axis=1, tiled=True)]
    unnamed x27 -> x29, local copies, waits for them, and re-layouts: 4.33 us -> 6.3 us
  transfers between devices with their start and end apart: 6 -> 5, of which waited for: 4 -> 3; matrix products, arithmetic and copies ran while one was open for 15% -> 14% of each run, Pallas kernels for 0% -> 0%
where the time goes in v1:
time: 307 us; the launch traced here: 306 us
  blocking collectives  109 us (36%)
  waiting for transfers between devices  72.4 us (24%)
  local copies, waits for them, and re-layouts  43.4 us (14%)
  matrix products  27 us (9%)
  other arithmetic  20.6 us (7%)
  starting transfers between devices  19.1 us (6%)
  between operations  14.5 us (5%)
    all_to_all x1, blocking collectives, inputs_cut(): all_to_all(jnp.stack([here_x for _ in range(psum(1, 'exp'))], axis=0), 'e...  53.2 us
    all_to_all x1, waiting for transfers between devices, body(): lax.all_to_all(partial_value, 'req', split_axis=0, concat_axis=0, tiled=T...  48.4 us
    dot_general x1, matrix products, body(): jnp.dot(active, w_down[0], preferred_element_type=jnp.float32)  16.4 us
    all_to_all x1, blocking collectives, body(): lax.all_to_all(pick_rows(page_rows, send_index, send_live), 'req', split_...  14.8 us
    psum x1, blocking collectives, body(): total_sq = lax.psum(squares, 'exp')  14.3 us
    all_to_all x1, waiting for transfers between devices, body(): lax.all_to_all(pick_rows(attention_out, send_index, send_live), 'req', sp...  13.7 us
    psum x1, blocking collectives, body(): lax.psum(jnp.dot(normed, router_w, precision=lax.Precision.HIGHEST), 'exp')  13.6 us
    all_to_all x1, blocking collectives, body(): lax.all_to_all(outgoing, 'req', split_axis=0, concat_axis=0, tiled=True)  12.9 us
  transfers between devices with their start and end apart: 5, of which 3 were waited for; matrix products, arithmetic and copies ran while one was open for 14% of the time, Pallas kernels for 0%

profile of v1, /device:TPU:0, one launch (start us, length us, event | category | flops | bytes accessed | tf_op | source)
XLA Modules:
  0.0 305.9 jit_solution(6368292855565957230)
XLA Ops:
  7.2 0.7 all-gather.2.cloned.1.call-update
  7.9 0.7 compare_select_fusion.1
  8.6 8.0 %scatter_custom_fusion = s32[2048]{0:T(1024)S(1)} fusion(s32[2048]{0:T(1024)S(1)} %compare_select_fusion.1, s32[2048]{0:T(1024)S(1)} %iota.72, s32[]{:T(128)} %constant.182.clone.1), kind=kCustom, calls=%fused_computation.93 | custom fusion | bytes 8196 | tf_op jit(solution)/shard_map/scatter | solution.py:61
  16.9 2.8 select_reduce_fusion
  20.7 1.6 gather_fusion.1
  22.4 0.7 select_select_fusion.4
  23.1 7.1 %all-to-all-start = ((bf16[16,4,512]{2,1,0:T(4,128)(2,1)}), bf16[16,4,512]{2,1,0:T(4,128)(2,1)S(1)}, u32[]{:S(2)}, u32[]{:S(2)}) async-start(bf16[16,4,512]{2,1,0:T(4,128)(2,1)} %select_select_fusion.4), calls=%async_computation | async-start | bytes 131072 | tf_op jit(solution)/shard_map/all_to_all | solution.py:98
  30.3 0.8 copy.126
  31.5 0.8 copy.136
  32.3 0.7 compare_and_fusion.2
  33.1 0.6 reduce-window.6
  34.6 0.8 compare_select_fusion.15
  35.3 1.1 gather_fusion
  37.7 0.4 broadcast_in_dim.228
  38.1 1.1 copy.138
  39.2 1.7 gather_fusion.5
  41.0 2.4 gather.47
  43.4 0.9 gather_fusion.6
  44.2 1.6 select_select_fusion
  45.8 0.9 gather_fusion.8
  46.8 1.0 select_select_fusion.1
  47.8 1.0 all_to_all.39
  48.8 0.8 compare_and_fusion.5
  49.6 7.2 %all-to-all-start.1 = ((bf16[16,4,4096]{2,1,0:T(4,128)(2,1)}), bf16[16,4,4096]{2,1,0:T(4,128)(2,1)S(1)}, u32[]{:S(2)}, u32[]{:S(2)}) async-start(bf16[16,4,4096]{2,1,0:T(4,128)(2,1)} %all_to_all.39), calls=%async_computation.1 | async-start | bytes 1048576 | tf_op jit(solution)/shard_map/all_to_all | solution.py:91
  57.3 0.8 gather_fusion.2
  58.2 13.7 %all-to-all-done.1 = bf16[16,4,4096]{2,1,0:T(4,128)(2,1)S(1)} async-done(((bf16[16,4,4096]{2,1,0:T(4,128)(2,1)}), bf16[16,4,4096]{2,1,0:T(4,128)(2,1)S(1)}, u32[]{:S(2)}, u32[]{:S(2)}) %all-to-all-start.1) | async-done | bytes 524320 | tf_op jit(solution)/shard_map/all_to_all | solution.py:91
  72.2 1.2 gather_fusion.7
  73.4 3.0 multiply_reduce_fusion
  76.4 14.3 %psum.14 = f32[128]{0:T(128)S(1)} all-reduce(f32[128]{0:T(128)S(1)} %get-tuple-element.14), channel_id=1, replica_groups=mesh['req'=16,'exp'=8] {'exp'}, use_global_device_ids=true, to_apply=%region_6.9 | all-reduce | flops 128 | bytes 1024 | tf_op jit(solution)/shard_map/psum | solution.py:134
  90.8 2.0 gather_fusion.3
  93.0 12.9 %all_to_all.56 = bf16[16,32,512]{2,1,0:T(8,128)(2,1)S(1)} all-to-all(bf16[16,32,512]{2,1,0:T(8,128)(2,1)S(1)} %select_select_fusion.3), channel_id=1, replica_groups=mesh['req'=16,'exp'=8] {'req'}, dimensions={0} | all-to-all | bytes 1048576 | tf_op jit(solution)/shard_map/all_to_all | solution.py:159
  106.5 53.2 %all_to_all.57 = bf16[8,512,512]{1,2,0:T(8,128)(2,1)S(1)} all-to-all(bf16[8,512,512]{1,2,0:T(8,128)(2,1)S(1)} %stack.5), channel_id=1, replica_groups=mesh['req'=16,'exp'=8] {'exp'}, dimensions={0} | all-to-all | bytes 8388608 | tf_op jit(solution)/shard_map/all_to_all | solution.py:16
  159.7 2.0 copy-done.5
  161.7 7.2 %fusion.4 = f32[512,896]{1,0:T(8,128)S(1)} fusion(bf16[512,4096]{0,1:T(8,128)(2,1)S(1)} %bitcast.71, bf16[1,4096,896]{2,1,0:T(8,128)(2,1)} %param.27), kind=kOutput, calls=%fused_computation.15 | convolution fusion | flops 3758096384 | bytes 13369344 | tf_op jit(solution)/shard_map/dot_general | solution.py:161
  168.9 16.4 %fusion.6 = bf16[512,4096]{1,0:T(8,128)(2,1)} fusion(bf16[1,896,4096]{2,1,0:T(8,128)(2,1)} %param.29, f32[512,896]{1,0:T(8,128)S(1)} %fusion.4, bf16[512,4096]{0,1:T(8,128)(2,1)} %bitcast.72, bf16[1,4096,896]{2,1,0:T(8,128)(2,1)} %param.28), kind=kOutput, calls=%fused_computation.17 | convolution fusion | flops 7521042432 | bytes 24903680 | tf_op jit(solution)/shard_map/dot_general | solution.py:165
  185.3 4.7 %all-to-all-start.4 = ((bf16[16,32,4096]{2,1,0:T(8,128)(2,1)}), bf16[16,32,4096]{2,1,0:T(8,128)(2,1)}, u32[]{:S(2)}, u32[]{:S(2)}) async-start(bf16[16,32,4096]{2,1,0:T(8,128)(2,1)} %bitcast.70), calls=%async_computation.4 | async-start | bytes 8388608 | tf_op jit(solution)/shard_map/all_to_all | solution.py:168
  190.8 13.6 %psum.15 = f32[128,8]{0,1:T(8,128)S(1)} all-reduce(f32[128,8]{0,1:T(8,128)S(1)} %fusion.26), channel_id=1, replica_groups=mesh['req'=16,'exp'=8] {'exp'}, use_global_device_ids=true, to_apply=%region_7.10 | all-reduce | flops 1024 | bytes 8192 | tf_op jit(solution)/shard_map/psum | solution.py:137
  204.5 48.4 %all-to-all-done.4 = bf16[16,32,4096]{2,1,0:T(8,128)(2,1)} async-done(((bf16[16,32,4096]{2,1,0:T(8,128)(2,1)}), bf16[16,32,4096]{2,1,0:T(8,128)(2,1)}, u32[]{:S(2)}, u32[]{:S(2)}) %all-to-all-start.4) | async-done | bytes 4194336 | tf_op jit(solution)/shard_map/all_to_all | solution.py:168
  252.9 6.6 %gather_fusion.4 = bf16[256,4096]{1,0:T(8,128)(2,1)S(1)} fusion(bf16[512,4096]{1,0:T(8,128)(2,1)} %bitcast.16, s32[1024]{0:T(1024)S(1)} %pad_clamp_fusion.1), kind=kCustom, calls=%fused_computation.8 | custom fusion | bytes 4195328 | tf_op jit(solution)/shard_map/jit(_take)/gather | solution.py:169
  259.5 2.7 gather.45
  262.1 4.0 %copy_select_fusion = bf16[128,2,4096]{2,0,1:T(8,128)(2,1)S(1)} fusion(bf16[128,2,4096]{2,1,0:T(2,128)(2,1)} %gather.45, pred[128,2]{0,1:T(4,128)(4,1)S(1)} %compare_and_fusion.3), kind=kLoop, calls=%fused_computation.22 | loop fusion | flops 1048576 | bytes 4194560 | tf_op jit(solution)/shard_map/jit(_take)/select_n | solution.py:169
  266.2 1.5 fusion.10
  267.9 14.8 %all_to_all.58 = bf16[16,4,4096]{2,1,0:T(4,128)(2,1)S(1)} all-to-all(bf16[16,4,4096]{2,1,0:T(4,128)(2,1)S(1)} %all_to_all.47), channel_id=1, replica_groups=mesh['req'=16,'exp'=8] {'req'}, dimensions={0} | all-to-all | bytes 1048576 | tf_op jit(solution)/shard_map/all_to_all | solution.py:105
  283.0 2.2 gather_fusion.9
  285.2 1.4 broadcast_select_fusion
  286.6 1.2 copy.139
  287.8 9.6 %reduce-scatter.2.cloned.1.call-done = bf16[128,512]{1,0:T(8,128)(2,1)} async-done(((bf16[128,4096]{1,0:T(8,128)(2,1)}), bf16[128,512]{1,0:T(8,128)(2,1)}) %reduce-scatter.2.cloned.1.call-update) | async-done | bytes 131088 | tf_op jit(solution)/shard_map/reduce_scatter | solution.py:173
  297.4 1.6 convert_add_fusion
  (101 shorter events, 6.9 us)
Async XLA Ops:
  7.2 32.1 %copy-start = (bf16[256,8,256]{2,1,0:T(8,128)(2,1)S(1)}, bf16[256,8,256]{2,1,0:T(8,128)(2,1)}, u32[]{:S(2)}) copy-start(bf16[256,8,256]{2,1,0:T(8,128)(2,1)} %param.22) | copy-start | bytes 3145732
  7.2 29.5 %copy-start.11 = (s32[128]{0:T(128)S(1)}, s32[128]{0:T(128)}, u32[]{:S(2)}) copy-start(s32[128]{0:T(128)} %param.24) | copy-start | bytes 1540
  7.2 66.2 %all-gather.2.cloned.1.call-start = ((), (), s32[]{:S(2)}) async-start(), calls=%async_computation.7 | async-start | bytes 4456448 | tf_op jit(solution)/shard_map/all_gather | solution.py:128
  23.1 26.5 %all-to-all-start = ((bf16[16,4,512]{2,1,0:T(4,128)(2,1)}), bf16[16,4,512]{2,1,0:T(4,128)(2,1)S(1)}, u32[]{:S(2)}, u32[]{:S(2)}) async-start(bf16[16,4,512]{2,1,0:T(4,128)(2,1)} %select_select_fusion.4), calls=%async_computation | async-start | bytes 131072 | tf_op jit(solution)/shard_map/all_to_all | solution.py:98
  39.2 4.1 %copy-start.4 = (bf16[128,4096]{1,0:T(8,128)(2,1)S(1)}, bf16[128,4096]{1,0:T(8,128)(2,1)}, u32[]{:S(2)}) copy-start(bf16[128,4096]{1,0:T(8,128)(2,1)} %param.17) | copy-start | bytes 3145732
  45.8 1.0 copy-start.2
  46.8 10.5 %copy-start.6 = (bf16[128,512]{1,0:T(8,128)(2,1)S(1)}, bf16[128,512]{1,0:T(8,128)(2,1)}, u32[]{:S(2)}) copy-start(bf16[128,512]{1,0:T(8,128)(2,1)} %param.18) | copy-start | bytes 393220
  49.6 22.2 %all-to-all-start.1 = ((bf16[16,4,4096]{2,1,0:T(4,128)(2,1)}), bf16[16,4,4096]{2,1,0:T(4,128)(2,1)S(1)}, u32[]{:S(2)}, u32[]{:S(2)}) async-start(bf16[16,4,4096]{2,1,0:T(4,128)(2,1)} %all_to_all.39), calls=%async_computation.1 | async-start | bytes 1048576 | tf_op jit(solution)/shard_map/all_to_all | solution.py:91
  73.4 17.4 %copy-start.10 = (f32[512]{0:T(512)S(1)}, f32[512]{0:T(512)}, u32[]{:S(2)}) copy-start(f32[512]{0:T(512)} %param.21) | copy-start | bytes 6148
  159.7 2.0 copy-start.5
  185.3 5.1 %copy-start.9 = (s32[128,2]{0,1:T(2,128)S(1)}, s32[128,2]{0,1:T(2,128)}, u32[]{:S(2)}) copy-start(s32[128,2]{0,1:T(2,128)} %param.26) | copy-start | bytes 3076
  185.3 5.2 %copy-start.8 = (f32[512,8]{0,1:T(8,128)S(1)}, f32[512,8]{0,1:T(8,128)}, u32[]{:S(2)}) copy-start(f32[512,8]{0,1:T(8,128)} %param.20) | copy-start | bytes 49156
  185.3 67.6 %all-to-all-start.4 = ((bf16[16,32,4096]{2,1,0:T(8,128)(2,1)}), bf16[16,32,4096]{2,1,0:T(8,128)(2,1)}, u32[]{:S(2)}, u32[]{:S(2)}) async-start(bf16[16,32,4096]{2,1,0:T(8,128)(2,1)} %bitcast.70), calls=%async_computation.4 | async-start | bytes 8388608 | tf_op jit(solution)/shard_map/all_to_all | solution.py:168
  189.9 107.5 %reduce-scatter.2.cloned.1.call-start = ((), (), s32[]{:S(2)}) async-start(), calls=%async_computation.8 | async-start | bytes 1179648 | tf_op jit(solution)/shard_map/reduce_scatter | solution.py:173
  266.2 1.5 copy-start.7
  267.6 15.2 %copy-start.3 = (bf16[128,4096]{1,0:T(8,128)(2,1)S(1)}, bf16[128,4096]{1,0:T(8,128)(2,1)}, u32[]{:S(2)}) copy-start(bf16[128,4096]{1,0:T(8,128)(2,1)} %copy-done.2) | copy-start | bytes 3145732
  283.0 16.1 %copy-start.1 = (bf16[256,8,256]{2,1,0:T(8,128)(2,1)S(1)}, bf16[256,8,256]{2,1,0:T(8,128)(2,1)}, u32[]{:S(2)}) copy-start(bf16[256,8,256]{2,1,0:T(8,128)(2,1)} %param.22) | copy-start | bytes 3145732
Sparse Core Ops, SparseCore 0:
  10.2 59.3 all-gather.1
  267.8 29.5 reduce-scatter.1
